TPU v7x, 256 devices: a whole 4x4x8 slice. The times are simulated.
256 devices in a mesh: pb: 16 (over z, core), kv: 16 (over y, x).
Axes of the slice: x: 4, y: 4, z: 8, core: 2. Of those that a mesh axis runs over, the one named last changes fastest.
Arguments:
- queries: bfloat16 [393216, 1024], P(('pb', 'kv')), may hold values from -8 to 8
- keys: bfloat16 [524288, 128], P(('kv', 'pb')), may hold values from -6 to 6
- values: bfloat16 [524288, 128], P(('kv', 'pb')), may hold values from -6 to 6
- selected: int32 [6144, 14], P(('pb', 'kv')), may hold values from 1 to 8190, as said below
Outputs:
- attended: bfloat16 [393216, 1024], P(('pb', 'kv'))
Inputs may be any that keep to these rules, and one draw needn't show every extreme that they name: `selected`: each row names 14 different blocks, never block 0 or block 8191. Key device k holds blocks k * 32 to (k + 1) * 32 - 1, devices counted with kv slowest; query device d holds query blocks d * 24 to (d + 1) * 24 - 1, devices counted with pb slowest. The query blocks of one device name together at most 2 distinct blocks of one key device, and in every draw some key device has exactly 2 named by every query device.
All inputs are finite; a program needn't handle non-finite values.
Results may differ from a plain program's by a relative error of at most 0.0046.
Values may be sent and summed in bfloat16 or wider, within the bound.
A program may use at most 128 MiB of HBM per device.

v0:
```python
import math
import jax
import jax.numpy as jnp
from jax import lax
from jax.sharding import PartitionSpec as P

H = 8
DH = 128
BLOCK = 64
TOPN = 16
QB = 64
CAP = 2


def holdings(wanted, owner, blocks_here):
    local_ids = owner * blocks_here + jnp.arange(blocks_here, dtype=jnp.int32)
    hits = (wanted[:, None] == local_ids[None, :]).astype(jnp.int32)
    present = jnp.max(hits, axis=0)
    return (present, jnp.cumsum(present) - present)


def slot_lists(present, slot_rank, slots):
    local_ids = jnp.arange(present.shape[-1], dtype=jnp.int32)
    slot_ids = jnp.arange(slots, dtype=jnp.int32)
    matches = (present[..., :, None] == 1) & (slot_rank[..., :, None] == slot_ids)
    return jnp.sum(jnp.where(matches, local_ids[:, None], 0), axis=-2)


def per_device(queries, keys, values, selected):
    pb_count = lax.axis_size("pb")
    kv_count = lax.axis_size("kv")
    devices = pb_count * kv_count
    blocks_here = keys.shape[0] // BLOCK
    query_blocks = queries.shape[0] // QB
    column_blocks = pb_count * blocks_here
    tiles_local = jnp.concatenate(
        [keys.reshape(blocks_here, BLOCK, DH), values.reshape(blocks_here, BLOCK, DH)], axis=2
    )
    column = lax.all_gather(tiles_local, "pb", axis=0, tiled=True)
    slots = CAP
    wanted = selected.reshape(-1)
    owners = jnp.arange(devices, dtype=jnp.int32)
    present, slot_rank = jax.vmap(lambda owner: holdings(wanted, owner, blocks_here))(owners)
    owner_lists = slot_lists(present, slot_rank, slots)
    by_column = (
        owner_lists.reshape(kv_count, pb_count, slots)
        + jnp.arange(pb_count, dtype=jnp.int32)[None, :, None] * blocks_here
    )
    by_column = by_column.reshape(kv_count, pb_count * slots)
    asked_for = lax.all_to_all(by_column, "kv", split_axis=0, concat_axis=0, tiled=True)
    me_kv = lax.axis_index("kv")
    end_pick = jnp.where(me_kv == kv_count - 1, column_blocks - 1, 0).astype(jnp.int32)
    picks = jnp.concatenate(
        [asked_for.reshape(kv_count, pb_count * slots), jnp.broadcast_to(end_pick, (kv_count, 1))],
        axis=1,
    )
    outgoing = jnp.take(column, picks.reshape(-1), axis=0).reshape(
        kv_count, pb_count * slots + 1, BLOCK, 2 * DH
    )
    fetched = lax.all_to_all(outgoing, "kv", split_axis=0, concat_axis=0, tiled=True)
    tile_table = fetched.reshape(devices * slots + kv_count, BLOCK, 2 * DH)
    owner_of = selected // blocks_here
    positions = owner_of * slots + jnp.take(slot_rank.reshape(-1), selected)
    positions = positions + owner_of // pb_count
    row = pb_count * slots + 1
    leading_positions = jnp.broadcast_to(
        jnp.array([row - 1, kv_count * row - 1], jnp.int32), (query_blocks, 2)
    )
    positions = jnp.concatenate([leading_positions, positions], axis=1)
    group_size = math.gcd(query_blocks, 8)
    q_groups = queries.reshape(query_blocks // group_size, group_size, QB * H, DH)
    p_groups = positions.reshape(query_blocks // group_size, group_size, TOPN)

    def attend(operands):
        q_block, positions_in = operands
        gathered = jnp.take(tile_table, positions_in.reshape(-1), axis=0).reshape(
            group_size, TOPN * BLOCK, 2 * DH
        )
        scores = jnp.einsum(
            "gqd,gkd->gqk", q_block, gathered[..., :DH], preferred_element_type=jnp.float32
        ) * DH ** (-0.5)
        weights = jnp.exp(scores - jnp.max(scores, axis=-1, keepdims=True))
        totals = jnp.sum(weights, axis=-1, keepdims=True)
        weighted = jnp.einsum(
            "gqk,gkd->gqd",
            weights.astype(jnp.bfloat16),
            gathered[..., DH:],
            preferred_element_type=jnp.float32,
        )
        return (weighted / totals).astype(jnp.bfloat16)

    result = lax.map(attend, (q_groups, p_groups))
    return result.reshape(query_blocks * QB, H * DH)


def solution(mesh):
    placed = (
        P(("pb", "kv"), None),
        P(("kv", "pb"), None),
        P(("kv", "pb"), None),
        P(("pb", "kv"), None),
    )
    return jax.shard_map(
        per_device, mesh=mesh, in_specs=placed, out_specs=P(("pb", "kv"), None), check_vma=False
    )
```

profile of v0, /device:TPU:1, one launch (start us, length us, event | category | flops | bytes accessed | tf_op | source)
XLA Modules:
  0.0 494.0 jit_solution(9905077446433948110)
XLA Ops:
  6.5 0.0 all-gather.2.cloned.1.call-start
  6.5 2.3 pad_maximum_fusion
  8.9 0.0 all-gather.2.cloned.1.call-update
  8.9 0.8 copy.30
  9.7 0.1 eq.42
  9.8 1.7 convert_reduce_fusion
  11.5 0.1 reduce_window_sum.11
  11.6 0.1 copy.38
  11.8 0.1 reshape.199
  11.9 0.1 add.109
  12.0 0.1 add.110
  12.1 0.6 broadcast_add_fusion
  12.7 7.6 %all-to-all-start = ((s32[16,1,32]{2,1,0:T(1,128)}), s32[16,1,32]{2,1,0:T(1,128)S(1)}, u32[]{:S(2)}, u32[]{:S(2)}) async-start(s32[16,1,32]{2,1,0:T(1,128)} %bitcast.6), calls=%async_computation | async-start | bytes 16384 | tf_op jit(solution)/shard_map/all_to_all | solution.py:50
  20.3 6.4 %all-to-all-done = s32[16,1,32]{2,1,0:T(1,128)S(1)} async-done(((s32[16,1,32]{2,1,0:T(1,128)}), s32[16,1,32]{2,1,0:T(1,128)S(1)}, u32[]{:S(2)}, u32[]{:S(2)}) %all-to-all-start) | async-done | bytes 2080 | tf_op jit(solution)/shard_map/all_to_all | solution.py:50
  26.7 0.1 reshape.202
  26.8 82.0 %all-gather.2.cloned.1.call-done = bf16[512,64,256]{2,1,0:T(8,128)(2,1)} async-done(((bf16[32,64,256]{2,1,0:T(8,128)(2,1)}), bf16[512,64,256]{2,1,0:T(8,128)(2,1)}) %all-gather.2.cloned.1.call-update) | async-done | bytes 16777232 | tf_op jit(solution)/shard_map/all_gather | solution.py:39
  108.9 21.2 %gather_fusion.2 = bf16[528,64,256]{2,1,0:T(8,128)(2,1)} fusion(bf16[512,64,256]{2,1,0:T(8,128)(2,1)} %all-gather.2.cloned.1.call-done, s32[1024]{0:T(1024)S(1)} %pad_clamp_fusion.1), kind=kCustom, calls=%fused_computation.2 | custom fusion | bytes 34605120 | tf_op jit(solution)/shard_map/jit(_take)/gather | solution.py:57
  130.1 14.4 %broadcast_select_fusion = bf16[16,33,64,256]{3,2,1,0:T(8,128)(2,1)} fusion(bf16[16,33,64,256]{3,2,1,0:T(8,128)(2,1)} %bitcast.37, pred[16,33]{1,0:T(8,128)(4,1)S(1)} %compare_and_fusion.1), kind=kLoop, calls=%fused_computation.26 | loop fusion | flops 8650752 | bytes 34603536 | tf_op jit(solution)/shard_map/jit(_take)/select_n | solution.py:57
  144.5 6.6 %all-to-all-start.1 = ((bf16[16,33,64,256]{3,2,1,0:T(8,128)(2,1)}), bf16[16,33,64,256]{3,2,1,0:T(8,128)(2,1)}, u32[]{:S(2)}, u32[]{:S(2)}) async-start(bf16[16,33,64,256]{3,2,1,0:T(8,128)(2,1)} %broadcast_select_fusion), calls=%async_computation.1 | async-start | bytes 34603008 | tf_op jit(solution)/shard_map/all_to_all | solution.py:60
  151.1 0.1 copy.37
  151.2 0.1 sub.31
  151.3 0.1 reshape.215
  151.4 0.0 copy-start
  151.5 2.5 gather_fusion.1
  154.0 0.1 reshape.214
  154.1 0.0 copy-done
  154.1 4.1 reshape.197
  158.3 0.1 add_bitcast_fusion
  158.4 251.6 %all-to-all-done.1 = bf16[16,33,64,256]{3,2,1,0:T(8,128)(2,1)} async-done(((bf16[16,33,64,256]{3,2,1,0:T(8,128)(2,1)}), bf16[16,33,64,256]{3,2,1,0:T(8,128)(2,1)}, u32[]{:S(2)}, u32[]{:S(2)}) %all-to-all-start.1) | async-done | bytes 17301536 | tf_op jit(solution)/shard_map/all_to_all | solution.py:60
  410.0 71.4 %while.10 = (s32[]{:T(128)}, bf16[3,8,512,128]{3,2,1,0:T(8,128)(2,1)}, bf16[3,8,512,128]{3,2,1,0:T(8,128)(2,1)S(1)}, s32[3,8,16]{2,1,0:T(8,128)S(1)}, bf16[528,64,256]{2,1,0:T(8,128)(2,1)}, /*index=5*/s32[]{:T(128)}) while((s32[]{:T(128)}, bf16[3,8,512,128]{3,2,1,0:T(8,128)(2,1)}, bf16[3,8,512,128]{3,2,1,0:T(8,128)(2,1)S(1)}, ...), condition=%wide.region_6.7_spmd, body=%wide.region_3.6_spmd.sunk | while | flops 2184177664 | bytes 73524040 | solution.py:92
  410.0 0.1 reshape.238
  410.1 8.7 %gather_fusion = bf16[128,64,256]{2,1,0:T(8,128)(2,1)} fusion(bf16[528,64,256]{2,1,0:T(8,128)(2,1)} %get-tuple-element.102, s32[1024]{0:T(1024)S(1)} %pad_clamp_fusion.4), kind=kCustom, calls=%fused_computation.clone.1 | custom fusion | bytes 8389120 | tf_op jit(solution)/shard_map/while/body/eval_jaxpr/jit(_take)/gather | solution.py:76
  418.8 0.1 broadcast_in_dim.86
  418.9 0.1 broadcast_in_dim.87
  419.0 4.6 bitcast_select_fusion.2
  423.6 2.4 multiply_reduce_fusion.2
  426.0 3.5 fusion.32
  429.5 4.3 bitcast_dynamic-update-slice_fusion.2
  433.8 0.1 reshape.238
  433.9 8.7 %gather_fusion = bf16[128,64,256]{2,1,0:T(8,128)(2,1)} fusion(bf16[528,64,256]{2,1,0:T(8,128)(2,1)} %get-tuple-element.102, s32[1024]{0:T(1024)S(1)} %pad_clamp_fusion.4), kind=kCustom, calls=%fused_computation.clone.1 | custom fusion | bytes 8389120 | tf_op jit(solution)/shard_map/while/body/eval_jaxpr/jit(_take)/gather | solution.py:76
  442.6 0.1 broadcast_in_dim.86
  442.7 0.1 broadcast_in_dim.87
  442.8 4.6 bitcast_select_fusion.2
  447.4 2.4 multiply_reduce_fusion.2
  449.8 3.5 fusion.32
  453.3 4.2 bitcast_dynamic-update-slice_fusion.2
  457.6 0.1 reshape.238
  457.7 8.7 %gather_fusion = bf16[128,64,256]{2,1,0:T(8,128)(2,1)} fusion(bf16[528,64,256]{2,1,0:T(8,128)(2,1)} %get-tuple-element.102, s32[1024]{0:T(1024)S(1)} %pad_clamp_fusion.4), kind=kCustom, calls=%fused_computation.clone.1 | custom fusion | bytes 8389120 | tf_op jit(solution)/shard_map/while/body/eval_jaxpr/jit(_take)/gather | solution.py:76
  466.4 0.1 broadcast_in_dim.86
  466.5 0.1 broadcast_in_dim.87
  466.6 4.6 bitcast_select_fusion.2
  471.1 2.4 multiply_reduce_fusion.2
  473.6 3.5 fusion.32
  477.1 4.2 bitcast_dynamic-update-slice_fusion.2
  481.4 5.8 %reshape.204 = bf16[1536,1024]{1,0:T(8,128)(2,1)} reshape(bf16[3,8,512,128]{3,2,1,0:T(8,128)(2,1)} %get-tuple-element.32) | data formatting | bytes 6291456 | tf_op jit(solution)/shard_map/reshape | solution.py:93
  (24 shorter events, 0.2 us)
Async XLA Ops:
  6.5 102.3 %all-gather.2.cloned.1.call-start = ((), (), s32[]{:S(2)}) async-start(), calls=%async_computation.2 | async-start | bytes 17825792 | tf_op jit(solution)/shard_map/all_gather | solution.py:39
  12.7 14.0 %all-to-all-start = ((s32[16,1,32]{2,1,0:T(1,128)}), s32[16,1,32]{2,1,0:T(1,128)S(1)}, u32[]{:S(2)}, u32[]{:S(2)}) async-start(s32[16,1,32]{2,1,0:T(1,128)} %bitcast.6), calls=%async_computation | async-start | bytes 16384 | tf_op jit(solution)/shard_map/all_to_all | solution.py:50
  144.5 265.4 %all-to-all-start.1 = ((bf16[16,33,64,256]{3,2,1,0:T(8,128)(2,1)}), bf16[16,33,64,256]{3,2,1,0:T(8,128)(2,1)}, u32[]{:S(2)}, u32[]{:S(2)}) async-start(bf16[16,33,64,256]{3,2,1,0:T(8,128)(2,1)} %broadcast_select_fusion), calls=%async_computation.1 | async-start | bytes 34603008 | tf_op jit(solution)/shard_map/all_to_all | solution.py:60
  151.4 2.7 copy-start
Sparse Core Ops, SparseCore 0:
  9.2 99.6 all-gather.1
where the time goes:
time: 495 us; the launch traced here: 494 us
  waiting for transfers between devices  340 us (69%)
  local copies, waits for them, and re-layouts  62.3 us (13%)
  other arithmetic  43.8 us (9%)
  matrix products  20 us (4%)
  starting transfers between devices  14.2 us (3%)
  between operations  13.6 us (3%)
    all_to_all x1, waiting for transfers between devices, per_device(): lax.all_to_all(outgoing, 'kv', split_axis=0, concat_axis=0, tiled=True)  252 us
    all_gather x1, waiting for transfers between devices, per_device(): column = lax.all_gather(tiles_local, 'pb', axis=0, tiled=True)  82 us
    gather x3, local copies, waits for them, and re-layouts, attend(): jnp.take(tile_table, positions_in.reshape(-1), axis=0)  26.1 us
    gather x1, local copies, waits for them, and re-layouts, per_device(): jnp.take(column, picks.reshape(-1), axis=0)  21.2 us
    select_n x2, other arithmetic, per_device(): jnp.take(column, picks.reshape(-1), axis=0)  14.5 us
    select_n x6, other arithmetic, attend(): jnp.take(tile_table, positions_in.reshape(-1), axis=0)  13.8 us
    dot_general x3, matrix products, attend(): jnp.einsum('gqk,gkd->gqd', weights.astype(jnp.bfloat16), gathered[..., DH...  12.7 us
    reduce_sum x3, other arithmetic, attend(): totals = jnp.sum(weights, axis=-1, keepdims=True)  10.6 us
  transfers between devices with their start and end apart: 3, of which 3 were waited for; matrix products, arithmetic and copies ran while one was open for 2% of the time, Pallas kernels for 0%

commit v1 on v0

--- a/solution.py
+++ b/solution.py
@@ -10,6 +10,11 @@
 TOPN = 16
 QB = 64
 CAP = 2
+
+
+def gather_by_exchange(x, axis, dim):
+    copies = jnp.concatenate([x] * lax.axis_size(axis), axis=dim)
+    return lax.all_to_all(copies, axis, dim, dim, tiled=True)
 
 
 def holdings(wanted, owner, blocks_here):
@@ -36,7 +41,7 @@
     tiles_local = jnp.concatenate(
         [keys.reshape(blocks_here, BLOCK, DH), values.reshape(blocks_here, BLOCK, DH)], axis=2
     )
-    column = lax.all_gather(tiles_local, "pb", axis=0, tiled=True)
+    column = gather_by_exchange(tiles_local, "pb", 0)
     slots = CAP
     wanted = selected.reshape(-1)
     owners = jnp.arange(devices, dtype=jnp.int32)

time: 495 us -> 786 us (1.59)
  waiting for transfers between devices: 340 us -> 611 us
  other arithmetic: 43.8 us -> 64.6 us
  between operations: 13.6 us -> 0.2 us
  starting transfers between devices: 14.2 us -> 24 us
    all_to_all x0 -> x1, waiting for transfers between devices: none -> 363 us  [gather_by_exchange(): return lax.all_to_all(copies, axis, dim, dim, tiled=True)]
    all_gather x1 -> x0, waiting for transfers between devices: 82 us -> none  [per_device(): column = lax.all_gather(tiles_local, 'pb', axis=0, tiled=True)]
    unnamed x0 -> x15, other arithmetic: none -> 21.9 us
    all_to_all x0 -> x1, starting transfers between devices: none -> 9.43 us  [gather_by_exchange(): return lax.all_to_all(copies, axis, dim, dim, tiled=True)]
  transfers between devices with their start and end apart: 3 -> 3, of which waited for: 3 -> 2; matrix products, arithmetic and copies ran while one was open for 2% -> 4% of each run, Pallas kernels for 0% -> 0%
where the time goes in v1:
time: 786 us; the launch traced here: 783 us
  waiting for transfers between devices  611 us (78%)
  other arithmetic  64.6 us (8%)
  local copies, waits for them, and re-layouts  62.4 us (8%)
  starting transfers between devices  24 us (3%)
  matrix products  20 us (3%)
    all_to_all x1, waiting for transfers between devices, gather_by_exchange(): return lax.all_to_all(copies, axis, dim, dim, tiled=True)  363 us
    all_to_all x1, waiting for transfers between devices, per_device(): lax.all_to_all(outgoing, 'kv', split_axis=0, concat_axis=0, tiled=True)  248 us
    gather x3, local copies, waits for them, and re-layouts, attend(): jnp.take(tile_table, positions_in.reshape(-1), axis=0)  26.1 us
    unnamed x15, other arithmetic  21.9 us
    gather x1, local copies, waits for them, and re-layouts, per_device(): jnp.take(column, picks.reshape(-1), axis=0)  21.2 us
  transfers between devices with their start and end apart: 3, of which 2 were waited for; matrix products, arithmetic and copies ran while one was open for 4% of the time, Pallas kernels for 0%

profile of v1, /device:TPU:1, one launch (start us, length us, event | category | flops | bytes accessed | tf_op | source)
XLA Modules:
  0.0 782.7 jit_solution(9958485853478510600)
XLA Ops:
  0.0 0.9 copy.30
  0.9 0.1 eq.42
  1.0 1.7 convert_reduce_fusion
  2.8 0.1 copy.38
  3.0 0.1 reshape.199
  3.2 0.1 add.110
  3.3 0.6 broadcast_add_fusion
  3.9 7.6 all-to-all-start
  11.5 2.3 constant_dynamic-update-slice_fusion.15
  13.8 2.4 constant_dynamic-update-slice_fusion.14
  16.2 2.3 constant_dynamic-update-slice_fusion.13
  18.5 2.3 constant_dynamic-update-slice_fusion.12
  20.8 1.1 constant_dynamic-update-slice_fusion.11
  22.0 1.2 constant_dynamic-update-slice_fusion.10
  23.1 1.1 constant_dynamic-update-slice_fusion.9
  24.3 1.1 constant_dynamic-update-slice_fusion.8
  25.4 1.2 constant_dynamic-update-slice_fusion.7
  26.6 1.1 constant_dynamic-update-slice_fusion.6
  27.7 1.1 constant_dynamic-update-slice_fusion.5
  28.9 1.1 constant_dynamic-update-slice_fusion.4
  30.0 1.2 constant_dynamic-update-slice_fusion.3
  31.2 1.1 constant_dynamic-update-slice_fusion.2
  32.3 1.1 constant_dynamic-update-slice_fusion.1
  33.4 1.1 constant_dynamic-update-slice_fusion
  34.6 9.4 %all-to-all-start.1 = ((bf16[512,64,256]{2,1,0:T(8,128)(2,1)}), bf16[512,64,256]{2,1,0:T(8,128)(2,1)}, u32[]{:S(2)}, u32[]{:S(2)}) async-start(bf16[512,64,256]{2,1,0:T(8,128)(2,1)} %constant_dynamic-update-slice_fusion), calls=%async_computation.1 | async-start | bytes 33554432 | tf_op jit(solution)/shard_map/all_to_all | solution.py:17
  44.0 0.1 reshape.202
  44.2 363.1 %all-to-all-done.1 = bf16[512,64,256]{2,1,0:T(8,128)(2,1)} async-done(((bf16[512,64,256]{2,1,0:T(8,128)(2,1)}), bf16[512,64,256]{2,1,0:T(8,128)(2,1)}, u32[]{:S(2)}, u32[]{:S(2)}) %all-to-all-start.1) | async-done | bytes 16777248 | tf_op jit(solution)/shard_map/all_to_all | solution.py:17
  407.3 21.2 %gather_fusion.2 = bf16[528,64,256]{2,1,0:T(8,128)(2,1)} fusion(bf16[512,64,256]{2,1,0:T(8,128)(2,1)} %all-to-all-done.1, s32[1024]{0:T(1024)S(1)} %pad_clamp_fusion.1), kind=kCustom, calls=%fused_computation.2 | custom fusion | bytes 34605120 | tf_op jit(solution)/shard_map/jit(_take)/gather | solution.py:62
  428.5 14.4 %broadcast_select_fusion = bf16[16,33,64,256]{3,2,1,0:T(8,128)(2,1)} fusion(bf16[16,33,64,256]{3,2,1,0:T(8,128)(2,1)} %bitcast.69, pred[16,33]{1,0:T(8,128)(4,1)S(1)} %compare_and_fusion.1), kind=kLoop, calls=%fused_computation.26 | loop fusion | flops 8650752 | bytes 34603536 | tf_op jit(solution)/shard_map/jit(_take)/select_n | solution.py:62
  442.9 7.0 all-to-all-start.2
  450.0 0.1 copy.37
  450.1 0.1 sub.31
  450.2 0.1 reshape.215
  450.3 2.5 gather_fusion.1
  452.8 0.1 reshape.214
  452.9 4.1 reshape.197
  457.1 0.1 add_bitcast_fusion
  457.2 248.3 %all-to-all-done.2 = bf16[16,33,64,256]{3,2,1,0:T(8,128)(2,1)} async-done(((bf16[16,33,64,256]{3,2,1,0:T(8,128)(2,1)}), bf16[16,33,64,256]{3,2,1,0:T(8,128)(2,1)}, u32[]{:S(2)}, u32[]{:S(2)}) %all-to-all-start.2) | async-done | bytes 17301536 | tf_op jit(solution)/shard_map/all_to_all | solution.py:65
  705.5 71.4 %while.10 = (s32[]{:T(128)}, bf16[3,8,512,128]{3,2,1,0:T(8,128)(2,1)}, bf16[3,8,512,128]{3,2,1,0:T(8,128)(2,1)S(1)}, s32[3,8,16]{2,1,0:T(8,128)S(1)}, bf16[528,64,256]{2,1,0:T(8,128)(2,1)}, /*index=5*/s32[]{:T(128)}) while((s32[]{:T(128)}, bf16[3,8,512,128]{3,2,1,0:T(8,128)(2,1)}, bf16[3,8,512,128]{3,2,1,0:T(8,128)(2,1)S(1)}, ...), condition=%wide.region_6.7_spmd, body=%wide.region_3.6_spmd.sunk | while | flops 2184177664 | bytes 73524040 | solution.py:97
  705.5 0.1 reshape.238
  705.6 8.7 %gather_fusion = bf16[128,64,256]{2,1,0:T(8,128)(2,1)} fusion(bf16[528,64,256]{2,1,0:T(8,128)(2,1)} %get-tuple-element.102, s32[1024]{0:T(1024)S(1)} %pad_clamp_fusion.4), kind=kCustom, calls=%fused_computation.clone.1 | custom fusion | bytes 8389120 | tf_op jit(solution)/shard_map/while/body/eval_jaxpr/jit(_take)/gather | solution.py:81
  714.3 0.1 broadcast_in_dim.86
  714.4 0.1 broadcast_in_dim.87
  714.5 4.6 bitcast_select_fusion.2
  719.1 2.4 multiply_reduce_fusion.2
  721.5 3.5 fusion.32
  725.1 4.3 bitcast_dynamic-update-slice_fusion.2
  729.3 0.1 reshape.238
  729.4 8.7 %gather_fusion = bf16[128,64,256]{2,1,0:T(8,128)(2,1)} fusion(bf16[528,64,256]{2,1,0:T(8,128)(2,1)} %get-tuple-element.102, s32[1024]{0:T(1024)S(1)} %pad_clamp_fusion.4), kind=kCustom, calls=%fused_computation.clone.1 | custom fusion | bytes 8389120 | tf_op jit(solution)/shard_map/while/body/eval_jaxpr/jit(_take)/gather | solution.py:81
  738.1 0.1 broadcast_in_dim.86
  738.2 0.1 broadcast_in_dim.87
  738.3 4.6 bitcast_select_fusion.2
  742.9 2.4 multiply_reduce_fusion.2
  745.3 3.5 fusion.32
  748.9 4.2 bitcast_dynamic-update-slice_fusion.2
  753.1 0.1 reshape.238
  753.2 8.7 %gather_fusion = bf16[128,64,256]{2,1,0:T(8,128)(2,1)} fusion(bf16[528,64,256]{2,1,0:T(8,128)(2,1)} %get-tuple-element.102, s32[1024]{0:T(1024)S(1)} %pad_clamp_fusion.4), kind=kCustom, calls=%fused_computation.clone.1 | custom fusion | bytes 8389120 | tf_op jit(solution)/shard_map/while/body/eval_jaxpr/jit(_take)/gather | solution.py:81
  761.9 0.1 broadcast_in_dim.86
  762.0 0.1 broadcast_in_dim.87
  762.1 4.6 bitcast_select_fusion.2
  766.7 2.4 multiply_reduce_fusion.2
  769.1 3.5 fusion.32
  772.7 4.2 bitcast_dynamic-update-slice_fusion.2
  776.9 5.8 reshape.204
  (33 shorter events, 0.4 us)
Async XLA Ops:
  0.0 20.8 %copy-start.1 = (bf16[2048,128]{1,0:T(8,128)(2,1)S(1)}, bf16[2048,128]{1,0:T(8,128)(2,1)}, u32[]{:S(2)}) copy-start(bf16[2048,128]{1,0:T(8,128)(2,1)} %param.8) | copy-start | bytes 1572868
  0.0 20.8 %copy-start = (bf16[2048,128]{1,0:T(8,128)(2,1)S(1)}, bf16[2048,128]{1,0:T(8,128)(2,1)}, u32[]{:S(2)}) copy-start(bf16[2048,128]{1,0:T(8,128)(2,1)} %param.9) | copy-start | bytes 1572868
  3.9 30.7 %all-to-all-start = ((s32[16,1,32]{2,1,0:T(1,128)}), s32[16,1,32]{2,1,0:T(1,128)S(1)}, u32[]{:S(2)}, u32[]{:S(2)}) async-start(s32[16,1,32]{2,1,0:T(1,128)} %bitcast.6), calls=%async_computation | async-start | bytes 16384 | tf_op jit(solution)/shard_map/all_to_all | solution.py:55
  34.6 372.7 %all-to-all-start.1 = ((bf16[512,64,256]{2,1,0:T(8,128)(2,1)}), bf16[512,64,256]{2,1,0:T(8,128)(2,1)}, u32[]{:S(2)}, u32[]{:S(2)}) async-start(bf16[512,64,256]{2,1,0:T(8,128)(2,1)} %constant_dynamic-update-slice_fusion), calls=%async_computation.1 | async-start | bytes 33554432 | tf_op jit(solution)/shard_map/all_to_all | solution.py:17
  442.9 262.6 %all-to-all-start.2 = ((bf16[16,33,64,256]{3,2,1,0:T(8,128)(2,1)}), bf16[16,33,64,256]{3,2,1,0:T(8,128)(2,1)}, u32[]{:S(2)}, u32[]{:S(2)}) async-start(bf16[16,33,64,256]{3,2,1,0:T(8,128)(2,1)} %broadcast_select_fusion), calls=%async_computation.2 | async-start | bytes 34603008 | tf_op jit(solution)/shard_map/all_to_all | solution.py:65
  449.9 3.0 copy-start.2
